TPU v7x, 32 devices: a whole 2x2x4 slice. The times are simulated.
32 devices in a mesh: rep: 8 (over y, x, core), fsdp: 4 (over z).
Axes of the slice: x: 2, y: 2, z: 4, core: 2. Of those that a mesh axis runs over, the one named last changes fastest.
Arguments:
- base: float32 [3, 32, 8192], P(None, 'fsdp'), may hold values from -6 to 6
- local: float32 [8, 3, 32, 8192], P('rep', None, 'fsdp'), may hold values from -6 to 6
- momentum: float32 [3, 32, 8192], P(None, 'fsdp', 'rep'), may hold values from -3 to 3
- hidden: bfloat16 [8, 512, 32], P('rep', 'fsdp'), may hold values from -6 to 6
- out_grad: bfloat16 [8, 512, 8192], P('rep', 'fsdp'), may hold values from -0.06591797 to 0.06591797
Outputs:
- mixed: float32 [8, 3, 32, 8192], P('rep', None, 'fsdp')
- momentum_out: float32 [3, 32, 8192], P(None, 'fsdp', 'rep')
- input_grad: bfloat16 [8, 512, 32], P('rep', 'fsdp')
- weight_grad: float32 [8, 32, 8192], P('rep', 'fsdp')
All inputs are finite; a program needn't handle non-finite values.
Results may differ from a plain program's by a relative error of at most 0.015.
Values may be sent and summed in bfloat16 or wider, within the bound.
No kernel may reach another device: no remote copies, remote signals or barrier semaphores. Data moves between devices by JAX's collectives and lax.ppermute only.
A program may use at most 64 MiB of HBM per device.

v0:
```python
import jax
import jax.numpy as jnp
from jax import lax
from jax.sharding import PartitionSpec as P

outer_beta = 0.9
outer_rate = 0.7
mix_keep = 0.5


def per_device(base, local, momentum, hidden, out_grad):
    replica_count = lax.axis_size("rep")
    weights = local[0, 2].astype(jnp.bfloat16)
    grads_here = out_grad[0]
    activations = hidden[0]
    input_grad = lax.dot_general(
        grads_here,
        lax.all_gather(weights, "fsdp", axis=0, tiled=True),
        (((1,), (1,)), ((), ())),
        preferred_element_type=jnp.float32,
    ).astype(jnp.bfloat16)
    weight_grad = lax.psum_scatter(
        lax.dot_general(
            activations, grads_here, (((0,), (0,)), ((), ())), preferred_element_type=jnp.float32
        ).astype(jnp.bfloat16),
        "fsdp",
        scatter_dimension=0,
        tiled=True,
    ).astype(jnp.float32)
    drift = base - local[0]
    share_width = momentum.shape[2]
    share_start = lax.axis_index("rep") * share_width
    delta = lax.psum(drift, "rep") / replica_count
    moment_all = lax.all_gather(momentum, "rep", axis=2, tiled=True)
    moment_new = outer_beta * moment_all + delta
    updated = base - outer_rate * (delta + outer_beta * moment_new)
    momentum_out = lax.dynamic_slice_in_dim(moment_new, share_start, share_width, 2)
    mixed = mix_keep * local[0] + (1.0 - mix_keep) * updated
    return (mixed[None], momentum_out, input_grad[None], weight_grad[None])


def solution(mesh):
    return jax.shard_map(
        per_device,
        mesh=mesh,
        in_specs=(
            P(None, "fsdp", None),
            P("rep", None, "fsdp", None),
            P(None, "fsdp", "rep"),
            P("rep", "fsdp", None),
            P("rep", "fsdp", None),
        ),
        out_specs=(
            P("rep", None, "fsdp", None),
            P(None, "fsdp", "rep"),
            P("rep", "fsdp", None),
            P("rep", "fsdp", None),
        ),
        check_vma=False,
    )
```

profile of v0, /device:TPU:0, one launch (start us, length us, event | category | flops | bytes accessed | tf_op | source)
XLA Modules:
  0.0 83.5 jit_solution(2399152442900048808)
XLA Ops:
  8.0 0.0 copy-start
  8.0 0.0 copy-start.3
  8.0 0.0 all-reduce.2.cloned.1.call-start
  8.1 2.5 %bitcast_subtract_fusion = f32[3,8,8192]{2,1,0:T(8,128)} fusion(f32[3,8,8192]{2,1,0:T(8,128)} %param.5, f32[1,3,8,8192]{3,2,1,0:T(8,128)} %param.6), kind=kLoop, calls=%fused_computation.7 | loop fusion | flops 196608 | bytes 2359296 | tf_op jit(solution)/shard_map/sub | solution.py:30
  10.5 0.0 copy-start.1
  10.5 0.0 copy-start.2
  10.5 0.0 all-reduce.2.cloned.1.call-update
  10.6 0.0 reduce-scatter.2.cloned.1.call-start
  10.6 0.0 copy-done
  10.6 0.0 copy-done.3
  10.6 1.2 %convolution_convert_fusion = bf16[32,8192]{1,0:T(8,128)(2,1)} fusion(bf16[1,128,8192]{2,1,0:T(8,128)(2,1)S(1)} %copy-done, bf16[1,128,32]{1,2,0:T(8,128)(2,1)S(1)} %copy-done.3), kind=kOutput, calls=%fused_computation | convolution fusion | flops 67371008 | bytes 2629632 | tf_op jit(solution)/shard_map/dot_general | solution.py:23
  11.8 0.0 reduce-scatter.2.cloned.1.call-update
  11.9 0.0 copy-done.1
  11.9 0.0 copy-done.2
  11.9 14.0 %all_gather.6 = f32[3,8,8192]{2,1,0:T(8,128)} all-gather(f32[3,8,1024]{2,1,0:T(8,128)S(1)} %copy-done.2), channel_id=1, replica_groups=mesh['rep'=8,'fsdp'=4] {'rep'}, dimensions={2}, use_global_device_ids=true | all-gather | bytes 884736 | tf_op jit(solution)/shard_map/all_gather | solution.py:34
  25.9 18.9 %all-gather = bf16[1,1,32,8192]{3,2,1,0:T(8,128)(2,1)S(1)} all-gather(bf16[1,1,8,8192]{3,2,1,0:T(8,128)(2,1)S(1)} %slice.7), channel_id=2, replica_groups=mesh['rep'=8,'fsdp'=4] {'fsdp'}, dimensions={2}, use_global_device_ids=true | all-gather | bytes 655360 | tf_op jit(solution)/shard_map/all_gather | solution.py:18
  44.8 1.4 %fusion.6 = bf16[1,128,32]{1,2,0:T(8,128)(2,1)} fusion(bf16[1,128,8192]{2,1,0:T(8,128)(2,1)S(1)} %copy-done, bf16[1,1,32,8192]{3,2,1,0:T(8,128)(2,1)S(1)} %all-gather), kind=kOutput, calls=%fused_computation.5 | convolution fusion | flops 67112960 | bytes 2629632 | tf_op jit(solution)/shard_map/dot_general | solution.py:16
  46.2 24.9 %all-reduce.2.cloned.1.call-done = f32[3,8,8192]{2,1,0:T(8,128)} async-done(((f32[3,8,8192]{2,1,0:T(8,128)}), f32[3,8,8192]{2,1,0:T(8,128)}) %all-reduce.2.cloned.1.call-update) | async-done | bytes 786448 | tf_op jit(solution)/shard_map/psum | solution.py:33
  71.1 2.7 %multiply_add_fusion = (f32[3,8,8192]{2,1,0:T(8,128)S(1)}, f32[1,3,8,8192]{3,2,1,0:T(8,128)}) fusion(f32[3,8,8192]{2,1,0:T(8,128)} %all_gather.6, f32[3,8,8192]{2,1,0:T(8,128)} %all-reduce.2.cloned.1.call-done, f32[3,8,8192]{2,1,0:T(8,128)} %param.5, f32[1,3,8,8192]{3,2,1,0:T(8,128)S(1)} %copy-done.1), kind=kLoop, calls=%fused_computation.10 | loop fusion | flops 1769472 | bytes 4718592 | tf_op jit(solution)/shard_map/add | solution.py:35
  73.8 0.6 constant_dynamic-slice_fusion
  74.5 0.0 reduce-scatter.2.cloned.1.call-done
  74.5 1.6 %bitcast_convert_fusion = f32[1,8,8192]{2,1,0:T(8,128)} fusion(bf16[8,8192]{1,0:T(8,128)(2,1)} %reduce-scatter.2.cloned.1.call-done), kind=kLoop, calls=%fused_computation.13 | loop fusion | flops 65536 | bytes 393216 | tf_op jit(solution)/shard_map/broadcast_in_dim | solution.py:39
  (1 shorter events, 0.0 us)
Async XLA Ops:
  8.0 2.6 %copy-start = (bf16[1,128,8192]{2,1,0:T(8,128)(2,1)S(1)}, bf16[1,128,8192]{2,1,0:T(8,128)(2,1)}, u32[]{:S(2)}) copy-start(bf16[1,128,8192]{2,1,0:T(8,128)(2,1)} %param.9) | copy-start | bytes 6291460
  8.0 2.6 %copy-start.3 = (bf16[1,128,32]{1,2,0:T(8,128)(2,1)S(1)}, bf16[1,128,32]{1,2,0:T(8,128)(2,1)}, u32[]{:S(2)}) copy-start(bf16[1,128,32]{1,2,0:T(8,128)(2,1)} %param.8) | copy-start | bytes 24580
  8.0 63.1 %all-reduce.2.cloned.1.call-start = ((), (), s32[]{:S(2)}) async-start(), calls=%async_computation.1 | async-start | bytes 1572864 | tf_op jit(solution)/shard_map/psum | solution.py:33
  10.5 1.3 %copy-start.1 = (f32[1,3,8,8192]{3,2,1,0:T(8,128)S(1)}, f32[1,3,8,8192]{3,2,1,0:T(8,128)}, u32[]{:S(2)}) copy-start(f32[1,3,8,8192]{3,2,1,0:T(8,128)} %param.6) | copy-start | bytes 2359300
  10.5 1.4 %copy-start.2 = (f32[3,8,1024]{2,1,0:T(8,128)S(1)}, f32[3,8,1024]{2,1,0:T(8,128)}, u32[]{:S(2)}) copy-start(f32[3,8,1024]{2,1,0:T(8,128)} %param.7) | copy-start | bytes 294916
  10.6 63.9 %reduce-scatter.2.cloned.1.call-start = ((), (), s32[]{:S(2)}) async-start(), calls=%async_computation.2 | async-start | bytes 655360 | tf_op jit(solution)/shard_map/reduce_scatter | solution.py:22
Sparse Core Ops, SparseCore 0:
  12.5 58.4 all-reduce.1
Sparse Core Ops, SparseCore 1:
  13.3 24.8 reduce-scatter.1
where the time goes:
time: 83.7 us; the launch traced here: 83.5 us
  blocking collectives  32.9 us (39%)
  waiting for transfers between devices  24.9 us (30%)
  between operations  15.5 us (19%)
  other arithmetic  6.82 us (8%)
  matrix products  2.62 us (3%)
    psum x1, waiting for transfers between devices, per_device(): delta = lax.psum(drift, 'rep') / replica_count  24.9 us
    all_gather x1, blocking collectives, per_device(): lax.all_gather(weights, 'fsdp', axis=0, tiled=True)  18.9 us
    all_gather x1, blocking collectives, per_device(): moment_all = lax.all_gather(momentum, 'rep', axis=2, tiled=True)  14 us
    add x1, other arithmetic, per_device(): moment_new = outer_beta * moment_all + delta  2.73 us
    sub x1, other arithmetic, per_device(): drift = base - local[0]  2.47 us
  transfers between devices with their start and end apart: 2, of which 1 were waited for; matrix products, arithmetic and copies ran while one was open for 7% of the time, Pallas kernels for 0%

commit v1 on v0

--- a/solution.py
+++ b/solution.py
@@ -30,7 +30,7 @@
     drift = base - local[0]
     share_width = momentum.shape[2]
     share_start = lax.axis_index("rep") * share_width
-    delta = lax.psum(drift, "rep") / replica_count
+    delta = jnp.sum(lax.all_gather(drift, "rep"), axis=0) / replica_count
     moment_all = lax.all_gather(momentum, "rep", axis=2, tiled=True)
     moment_new = outer_beta * moment_all + delta
     updated = base - outer_rate * (delta + outer_beta * moment_new)

time: 83.7 us -> 77.7 us (0.928)
  waiting for transfers between devices: 24.9 us -> 14.7 us
  other arithmetic: 6.82 us -> 10.5 us
  blocking collectives: 32.9 us -> 31 us
  local copies, waits for them, and re-layouts: 0.68 us -> 2.2 us
    psum x1 -> x0, waiting for transfers between devices: 24.9 us -> none  [per_device(): delta = lax.psum(drift, 'rep') / replica_count]
    all_gather x0 -> x1, waiting for transfers between devices: none -> 14.7 us  [per_device(): delta = jnp.sum(lax.all_gather(drift, 'rep'), axis=0) / replica_count]
    reduce_sum x0 -> x1, other arithmetic: none -> 4.05 us  [per_device(): delta = jnp.sum(lax.all_gather(drift, 'rep'), axis=0) / replica_count]
    unnamed x8 -> x6, local copies, waits for them, and re-layouts: 0.02 us -> 1.54 us
    all_gather x1, blocking collectives: 14 us -> 12.9 us  [per_device(): moment_all = lax.all_gather(momentum, 'rep', axis=2, tiled=True)]
where the time goes in v1:
time: 77.7 us; the launch traced here: 77.4 us
  blocking collectives  31 us (40%)
  between operations  15.5 us (20%)
  waiting for transfers between devices  14.7 us (19%)
  other arithmetic  10.5 us (14%)
  matrix products  3.33 us (4%)
  local copies, waits for them, and re-layouts  2.2 us (3%)
    all_gather x1, blocking collectives, per_device(): lax.all_gather(weights, 'fsdp', axis=0, tiled=True)  18.1 us
    all_gather x1, waiting for transfers between devices, per_device(): delta = jnp.sum(lax.all_gather(drift, 'rep'), axis=0) / replica_count  14.7 us
    all_gather x1, blocking collectives, per_device(): moment_all = lax.all_gather(momentum, 'rep', axis=2, tiled=True)  12.9 us
    reduce_sum x1, other arithmetic, per_device(): delta = jnp.sum(lax.all_gather(drift, 'rep'), axis=0) / replica_count  4.05 us
    add x1, other arithmetic, per_device(): moment_new = outer_beta * moment_all + delta  2.73 us
    sub x1, other arithmetic, per_device(): drift = base - local[0]  2.1 us
    dot_general x1, matrix products, per_device(): lax.dot_general(activations, grads_here, (((0,), (0,)), ((), ())), prefer...  1.91 us
    broadcast_in_dim x1, other arithmetic, per_device(): return (mixed[None], momentum_out, input_grad[None], weight_grad[None])  1.62 us
  transfers between devices with their start and end apart: 2, of which 1 were waited for; matrix products, arithmetic and copies ran while one was open for 7% of the time, Pallas kernels for 0%

profile of v1, /device:TPU:0, one launch (start us, length us, event | category | flops | bytes accessed | tf_op | source)
XLA Modules:
  0.0 77.4 jit_solution(1409896118322770474)
XLA Ops:
  8.0 0.0 copy-start
  8.0 0.0 copy-start.1
  8.0 0.0 reduce-scatter.2.cloned.1.call-start
  8.1 1.5 %copy-done = bf16[1,128,8192]{2,1,0:T(8,128)(2,1)S(1)} copy-done((bf16[1,128,8192]{2,1,0:T(8,128)(2,1)S(1)}, bf16[1,128,8192]{2,1,0:T(8,128)(2,1)}, u32[]{:S(2)}) %copy-start) | copy-done | bytes 2097176
  9.6 1.9 %convolution_convert_fusion = bf16[32,8192]{1,0:T(8,128)(2,1)} fusion(bf16[1,128,8192]{2,1,0:T(8,128)(2,1)S(1)} %copy-done, bf16[1,128,32]{1,2,0:T(8,128)(2,1)} %param.8), kind=kOutput, calls=%fused_computation | convolution fusion | flops 67371008 | bytes 2629632 | tf_op jit(solution)/shard_map/dot_general | solution.py:23
  11.5 0.0 copy-start.2
  11.5 0.0 reduce-scatter.2.cloned.1.call-update
  11.5 0.0 all-gather.4.cloned.1.call-start
  11.6 0.0 copy-done.1
  11.6 2.1 %bitcast_subtract_fusion = f32[3,8,8192]{2,1,0:T(8,128)} fusion(f32[3,8,8192]{2,1,0:T(8,128)} %param.5, f32[1,3,8,8192]{3,2,1,0:T(8,128)S(1)} %copy-done.1), kind=kLoop, calls=%fused_computation.7 | loop fusion | flops 196608 | bytes 2359296 | tf_op jit(solution)/shard_map/sub | solution.py:30
  13.7 0.0 all-gather.4.cloned.1.call-update
  13.7 0.0 copy-done.2
  13.8 12.9 %all_gather.14 = f32[3,8,8192]{2,1,0:T(8,128)} all-gather(f32[3,8,1024]{2,1,0:T(8,128)S(1)} %copy-done.2), channel_id=1, replica_groups=mesh['rep'=8,'fsdp'=4] {'rep'}, dimensions={2}, use_global_device_ids=true | all-gather | bytes 884736 | tf_op jit(solution)/shard_map/all_gather | solution.py:34
  26.7 18.1 %all-gather.1 = bf16[1,1,32,8192]{3,2,1,0:T(8,128)(2,1)S(1)} all-gather(bf16[1,1,8,8192]{3,2,1,0:T(8,128)(2,1)S(1)} %slice.7), channel_id=3, replica_groups=mesh['rep'=8,'fsdp'=4] {'fsdp'}, dimensions={2}, use_global_device_ids=true | all-gather | bytes 655360 | tf_op jit(solution)/shard_map/all_gather | solution.py:18
  44.8 1.4 %fusion.6 = bf16[1,128,32]{1,2,0:T(8,128)(2,1)} fusion(bf16[1,128,8192]{2,1,0:T(8,128)(2,1)S(1)} %copy-done, bf16[1,1,32,8192]{3,2,1,0:T(8,128)(2,1)S(1)} %all-gather.1), kind=kOutput, calls=%fused_computation.5 | convolution fusion | flops 67112960 | bytes 2629632 | tf_op jit(solution)/shard_map/dot_general | solution.py:16
  46.2 0.0 reduce-scatter.2.cloned.1.call-done
  46.2 1.6 %bitcast_convert_fusion = f32[1,8,8192]{2,1,0:T(8,128)} fusion(bf16[8,8192]{1,0:T(8,128)(2,1)} %reduce-scatter.2.cloned.1.call-done), kind=kLoop, calls=%fused_computation.13 | loop fusion | flops 65536 | bytes 393216 | tf_op jit(solution)/shard_map/broadcast_in_dim | solution.py:39
  47.8 14.7 %all-gather.4.cloned.1.call-done = f32[24,8,8192]{2,1,0:T(8,128)} async-done(((f32[3,8,8192]{2,1,0:T(8,128)}), f32[24,8,8192]{2,1,0:T(8,128)}) %all-gather.4.cloned.1.call-update) | async-done | bytes 6291472 | tf_op jit(solution)/shard_map/all_gather | solution.py:33
  62.5 4.1 %reduce_sum.9 = f32[3,8,8192]{2,1,0:T(8,128)} reduce(f32[8,3,8,8192]{3,2,1,0:T(8,128)} %bitcast.30, f32[]{:T(128)} %constant.3.clone.1), dimensions={0}, to_apply=%region_0.0 | reduce | flops 1376256 | bytes 7077892 | tf_op jit(solution)/shard_map/reduce_sum | solution.py:33
  66.6 2.7 %multiply_add_fusion = (f32[3,8,8192]{2,1,0:T(8,128)S(1)}, f32[1,3,8,8192]{3,2,1,0:T(8,128)}) fusion(f32[3,8,8192]{2,1,0:T(8,128)} %all_gather.14, f32[3,8,8192]{2,1,0:T(8,128)} %reduce_sum.9, f32[3,8,8192]{2,1,0:T(8,128)} %param.5, f32[1,3,8,8192]{3,2,1,0:T(8,128)S(1)} %copy-done.1), kind=kLoop, calls=%fused_computation.10 | loop fusion | flops 1769472 | bytes 4718592 | tf_op jit(solution)/shard_map/add | solution.py:35
  69.3 0.6 constant_dynamic-slice_fusion
  (1 shorter events, 0.0 us)
Async XLA Ops:
  8.0 1.6 %copy-start = (bf16[1,128,8192]{2,1,0:T(8,128)(2,1)S(1)}, bf16[1,128,8192]{2,1,0:T(8,128)(2,1)}, u32[]{:S(2)}) copy-start(bf16[1,128,8192]{2,1,0:T(8,128)(2,1)} %param.9) | copy-start | bytes 6291460
  8.0 3.6 %copy-start.1 = (f32[1,3,8,8192]{3,2,1,0:T(8,128)S(1)}, f32[1,3,8,8192]{3,2,1,0:T(8,128)}, u32[]{:S(2)}) copy-start(f32[1,3,8,8192]{3,2,1,0:T(8,128)} %param.6) | copy-start | bytes 2359300
  8.0 38.2 %reduce-scatter.2.cloned.1.call-start = ((), (), s32[]{:S(2)}) async-start(), calls=%async_computation.1 | async-start | bytes 655360 | tf_op jit(solution)/shard_map/reduce_scatter | solution.py:22
  11.5 2.2 %copy-start.2 = (f32[3,8,1024]{2,1,0:T(8,128)S(1)}, f32[3,8,1024]{2,1,0:T(8,128)}, u32[]{:S(2)}) copy-start(f32[3,8,1024]{2,1,0:T(8,128)} %param.7) | copy-start | bytes 294916
  11.5 51.0 %all-gather.4.cloned.1.call-start = ((), (), s32[]{:S(2)}) async-start(), calls=%async_computation.2 | async-start | bytes 7077888 | tf_op jit(solution)/shard_map/all_gather | solution.py:33
Sparse Core Ops, SparseCore 0:
  11.7 26.2 reduce-scatter.1
Sparse Core Ops, SparseCore 1:
  14.5 48.0 all-gather.3
